TPU v7x, 32 devices: a whole 2x2x4 slice. The times are simulated.
32 devices in a mesh: bin: 8 (over y, x, core), shard: 4 (over z).
Axes of the slice: x: 2, y: 2, z: 4, core: 2. Of those that a mesh axis runs over, the one named last changes fastest.
Arguments:
- block_input: bfloat16 [16384, 1152], P(('bin', 'shard')), may hold values from -6 to 6
- label_embed: float32 [64, 1152], P('bin'), may hold values from -6 to 6
- time_index: int32 [64], P('bin'), may hold values from 0 to 999
- segment_ids: int32 [16384], P('bin'), may hold values from 0 to 7, as said below
- ada_weight: bfloat16 [1152, 6912], replicated, may hold values from -0.1875 to 0.1875
- ada_bias: float32 [6912], replicated, may hold values from -2 to 2
- qkv_weight: bfloat16 [1152, 3456], P('bin', 'shard'), may hold values from -0.1875 to 0.1875
- qv_bias: float32 [2304], replicated, may hold values from -2 to 2
- proj_weight: bfloat16 [1152, 1152], P('bin', 'shard'), may hold values from -0.75 to 0.75
- proj_bias: float32 [1152], replicated, may hold values from -2 to 2
- up_weight: bfloat16 [1152, 4608], P('bin', 'shard'), may hold values from -0.1875 to 0.1875
- up_bias: float32 [4608], replicated, may hold values from -2 to 2
- down_weight: bfloat16 [4608, 1152], P('bin', 'shard'), may hold values from -0.09375 to 0.09375
- down_bias: float32 [1152], replicated, may hold values from -2 to 2
- bin_weight: float32 [8], P('bin'), may hold values from 0.3 to 3
- out_cotangent: bfloat16 [16384, 1152], P(('bin', 'shard')), may hold values from -6 to 6
Outputs:
- block_output: float32 [16384, 1152], P(('bin', 'shard'))
- grad_input: float32 [16384, 1152], P(('bin', 'shard'))
- grad_label: float32 [64, 1152], P('bin')
- grad_ada_weight: float32 [1152, 6912], P(None, ('bin', 'shard'))
- grad_ada_bias: float32 [6912], P(('bin', 'shard'))
- grad_qkv_weight: float32 [1152, 3456], P('bin', 'shard')
- grad_qv_bias: float32 [2304], replicated
- grad_proj_weight: float32 [1152, 1152], P('bin', 'shard')
- grad_proj_bias: float32 [1152], replicated
- grad_up_weight: float32 [1152, 4608], P('bin', 'shard')
- grad_up_bias: float32 [4608], replicated
- grad_down_weight: float32 [4608, 1152], P('bin', 'shard')
- grad_down_bias: float32 [1152], replicated
Inputs may be any that keep to these rules, and one draw needn't show every extreme that they name: `segment_ids`: within each bin's group of 2048 tokens the ids number its images from 0 in order of their tokens; every image is 256 or 1024 consecutive tokens, and both sizes occur in every draw. Slots at or above a group's image count are unused.
All inputs are finite; a program needn't handle non-finite values.
Results may differ from a plain program's by a relative error of at most 0.017.
Values may be sent and summed in bfloat16 or wider, within the bound.
No kernel may reach another device: no remote copies, remote signals or barrier semaphores. Data moves between devices by JAX's collectives and lax.ppermute only.
A program may use at most 384 MiB of HBM per device.

v0:
```python
import math

import jax
import jax.numpy as jnp
from jax import lax
from jax.sharding import PartitionSpec as P

HEADS = 16
HEAD_DIM = 72


def time_embed(time_index, width):
    half_width = width // 2
    freqs = jnp.exp(-math.log(10000.0) * jnp.arange(half_width, dtype=jnp.float32) / half_width)
    angles = time_index.astype(jnp.float32)[:, None] * freqs[None, :]
    return jnp.concatenate([jnp.cos(angles), jnp.sin(angles)], axis=1)


def layer_norm(value):
    center = value - jnp.mean(value, axis=1, keepdims=True)
    inverse = lax.rsqrt(jnp.mean(center * center, axis=1, keepdims=True) + 1e-06)
    return (center * inverse, inverse)


def norm_back(normed, inverse, grad_normed):
    mean_grad = jnp.mean(grad_normed, axis=1, keepdims=True)
    mean_cross = jnp.mean(grad_normed * normed, axis=1, keepdims=True)
    return inverse * (grad_normed - mean_grad - normed * mean_cross)


def matmul(left, right):
    return jnp.dot(left, right, preferred_element_type=jnp.float32)


def contract_rows(left, right):
    return lax.dot_general(
        left, right, (((0,), (0,)), ((), ())), preferred_element_type=jnp.float32
    )


def contract_cols(left, right):
    return lax.dot_general(
        left, right, (((1,), (1,)), ((), ())), preferred_element_type=jnp.float32
    )


def head_blocks(matrix):
    group_heads = 4
    return matrix.reshape(matrix.shape[0], HEADS // group_heads, group_heads, HEAD_DIM).transpose(
        1, 0, 2, 3
    )


def merge_heads(blocks):
    return blocks.transpose(1, 0, 2, 3).reshape(blocks.shape[1], -1)


def block_scores(query, keys, same):
    scores = jnp.einsum("qhd,khd->hqk", query, keys, preferred_element_type=jnp.float32)
    scores = scores * (1.0 / math.sqrt(HEAD_DIM))
    return jnp.where(same[None], scores, -1e30)


def attend_forward(query_low, keys_all, values_all, same):

    def one_block(operands):
        query, keys, values = operands
        scores = block_scores(query, keys, same)
        top = jnp.max(scores, axis=2, keepdims=True)
        expo = jnp.exp(scores - top)
        total = jnp.sum(expo, axis=2, keepdims=True)
        probs = (expo / total).astype(jnp.bfloat16)
        output = jnp.einsum("hqk,khd->qhd", probs, values, preferred_element_type=jnp.float32)
        return (output, (top + jnp.log(total))[:, :, 0])

    outputs, log_total = lax.map(
        one_block, (head_blocks(query_low), head_blocks(keys_all), head_blocks(values_all))
    )
    return (merge_heads(outputs), log_total)


def attend_backward(query_low, keys_all, values_all, same, log_total, grad_heads):
    scale = 1.0 / math.sqrt(HEAD_DIM)

    def one_block(operands):
        query, keys, values, log_block, grad_block = operands
        scores = block_scores(query, keys, same)
        probs = jnp.exp(scores - log_block[:, :, None])
        grad_probs = jnp.einsum(
            "qhd,khd->hqk", grad_block, values, preferred_element_type=jnp.float32
        )
        delta = jnp.sum(grad_probs * probs, axis=2, keepdims=True)
        grad_scores = (probs * (grad_probs - delta)).astype(jnp.bfloat16)
        grad_query = (
            jnp.einsum("hqk,khd->qhd", grad_scores, keys, preferred_element_type=jnp.float32)
            * scale
        )
        grad_keys = (
            jnp.einsum("hqk,qhd->khd", grad_scores, query, preferred_element_type=jnp.float32)
            * scale
        )
        grad_values = jnp.einsum(
            "hqk,qhd->khd",
            probs.astype(jnp.bfloat16),
            grad_block,
            preferred_element_type=jnp.float32,
        )
        return (grad_query, grad_keys, grad_values)

    grad_query, grad_keys, grad_values = lax.map(
        one_block,
        (
            head_blocks(query_low),
            head_blocks(keys_all),
            head_blocks(values_all),
            log_total,
            head_blocks(grad_heads),
        ),
    )
    return (merge_heads(grad_query), merge_heads(grad_keys), merge_heads(grad_values))


def collect_weights(local_weights):
    wider = (
        lax.all_gather(local_weights[0], "shard", axis=1, tiled=True),
        lax.all_gather(local_weights[1], "shard", axis=1, tiled=True),
        lax.all_gather(local_weights[2], "shard", axis=1, tiled=True),
        lax.all_gather(local_weights[3], "shard", axis=1, tiled=True),
    )
    return (
        lax.all_gather(wider[0], "bin", axis=0, tiled=True),
        lax.all_gather(wider[1], "bin", axis=0, tiled=True),
        lax.all_gather(wider[2], "bin", axis=0, tiled=True),
        lax.all_gather(wider[3], "bin", axis=0, tiled=True),
    )


def forward_pass(full_weights, tokens, per_token, biases, segment_ids, own_segments):
    qkv_full, proj_full, up_full, down_full = full_weights
    qv_bias, proj_bias, up_bias, down_bias = biases
    width = tokens.shape[1]
    shift_a, scale_a, gate_a, shift_m, scale_m, gate_m = jnp.split(per_token, 6, axis=1)
    normed, inverse = layer_norm(tokens)
    attn_in = (normed * (1.0 + scale_a) + shift_a).astype(jnp.bfloat16)
    qkv_bias = jnp.concatenate([qv_bias[:width], jnp.zeros((width,), jnp.float32), qv_bias[width:]])
    qkv_low = (matmul(attn_in, qkv_full) + qkv_bias).astype(jnp.bfloat16)
    query_low = qkv_low[:, :width]
    keys_all, values_all = (
        lax.all_gather(qkv_low[:, width : 2 * width], "shard", axis=0, tiled=True),
        lax.all_gather(qkv_low[:, 2 * width :], "shard", axis=0, tiled=True),
    )
    same = own_segments[:, None] == segment_ids[None, :]
    heads_out, log_total = attend_forward(query_low, keys_all, values_all, same)
    heads_low = heads_out.astype(jnp.bfloat16)
    attn_out = matmul(heads_low, proj_full) + proj_bias
    middle = tokens + gate_a * attn_out
    normed_mlp, inverse_mlp = layer_norm(middle)
    mlp_in = (normed_mlp * (1.0 + scale_m) + shift_m).astype(jnp.bfloat16)
    pre_act = matmul(mlp_in, up_full) + up_bias
    act_low = jax.nn.gelu(pre_act, approximate=True).astype(jnp.bfloat16)
    mlp_out = matmul(act_low, down_full) + down_bias
    result = middle + gate_m * mlp_out
    saved = (
        normed,
        inverse,
        attn_in,
        query_low,
        keys_all,
        values_all,
        log_total,
        heads_low,
        attn_out,
        normed_mlp,
        inverse_mlp,
        mlp_in,
        pre_act,
        act_low,
        mlp_out,
        same,
    )
    return (result, saved)


def per_device(
    block_input,
    label_embed,
    time_index,
    segment_ids,
    ada_weight,
    ada_bias,
    qkv_weight,
    qv_bias,
    proj_weight,
    proj_bias,
    up_weight,
    up_bias,
    down_weight,
    down_bias,
    bin_weight,
    out_cotangent,
):
    tokens = block_input.astype(jnp.float32)
    width = tokens.shape[1]
    tok_count = tokens.shape[0]
    slots = label_embed.shape[0]
    own_segments = lax.dynamic_slice_in_dim(
        segment_ids, lax.axis_index("shard") * tok_count, tok_count
    )
    onehot = (own_segments[:, None] == jnp.arange(slots, dtype=jnp.int32)[None, :]).astype(
        jnp.float32
    )
    cond = label_embed + time_embed(time_index, width)
    cond_low = jax.nn.silu(cond).astype(jnp.bfloat16)
    modul = matmul(cond_low, ada_weight) + ada_bias
    per_token = jnp.dot(
        onehot, modul, precision=lax.Precision.HIGHEST, preferred_element_type=jnp.float32
    )
    biases = (qv_bias, proj_bias, up_bias, down_bias)
    local_weights = (qkv_weight, proj_weight, up_weight, down_weight)
    full_weights = collect_weights(local_weights)
    result, saved = forward_pass(full_weights, tokens, per_token, biases, segment_ids, own_segments)
    grad_out = out_cotangent.astype(jnp.float32) * bin_weight[0]
    local_again, tokens_again, per_token_again, grad_out = lax.optimization_barrier(
        (local_weights, tokens, per_token, grad_out)
    )
    full_weights = collect_weights(local_again)
    saved = forward_pass(
        full_weights, tokens_again, per_token_again, biases, segment_ids, own_segments
    )[1]
    (
        normed,
        inverse,
        attn_in,
        query_low,
        keys_all,
        values_all,
        log_total,
        heads_low,
        attn_out,
        normed_mlp,
        inverse_mlp,
        mlp_in,
        pre_act,
        act_low,
        mlp_out,
        same,
    ) = saved
    qkv_full, proj_full, up_full, down_full = full_weights
    shift_a, scale_a, gate_a, shift_m, scale_m, gate_m = jnp.split(per_token, 6, axis=1)
    grad_mlp = (grad_out * gate_m).astype(jnp.bfloat16)
    grad_down_w = contract_rows(act_low, grad_mlp)
    grad_down_b = jnp.sum(grad_mlp.astype(jnp.float32), axis=0)
    grad_act = contract_cols(grad_mlp, down_full)
    gelu_back = jax.vjp(lambda value: jax.nn.gelu(value, approximate=True), pre_act)[1]
    grad_pre = gelu_back(grad_act)[0].astype(jnp.bfloat16)
    grad_up_w = contract_rows(mlp_in, grad_pre)
    grad_up_b = jnp.sum(grad_pre.astype(jnp.float32), axis=0)
    grad_in_mlp = contract_cols(grad_pre, up_full)
    grad_mid = grad_out + norm_back(normed_mlp, inverse_mlp, grad_in_mlp * (1.0 + scale_m))
    grad_attn = (grad_mid * gate_a).astype(jnp.bfloat16)
    grad_proj_w = contract_rows(heads_low, grad_attn)
    grad_proj_b = jnp.sum(grad_attn.astype(jnp.float32), axis=0)
    grad_heads = contract_cols(grad_attn, proj_full).astype(jnp.bfloat16)
    grad_query, grad_keys_all, grad_values_all = attend_backward(
        query_low, keys_all, values_all, same, log_total, grad_heads
    )
    grad_keys, grad_values = (
        lax.psum_scatter(
            grad_keys_all.astype(jnp.bfloat16), "shard", scatter_dimension=0, tiled=True
        ).astype(jnp.float32),
        lax.psum_scatter(
            grad_values_all.astype(jnp.bfloat16), "shard", scatter_dimension=0, tiled=True
        ).astype(jnp.float32),
    )
    grad_qkv = jnp.concatenate(
        [
            grad_query.astype(jnp.bfloat16),
            grad_keys.astype(jnp.bfloat16),
            grad_values.astype(jnp.bfloat16),
        ],
        axis=1,
    )
    grad_qkv_w = contract_rows(attn_in, grad_qkv)
    grad_qkv_wide = grad_qkv.astype(jnp.float32)
    grad_qv_b = jnp.concatenate(
        [jnp.sum(grad_qkv_wide[:, :width], axis=0), jnp.sum(grad_qkv_wide[:, 2 * width :], axis=0)]
    )
    grad_in_attn = contract_cols(grad_qkv, qkv_full)
    grad_input = grad_mid + norm_back(normed, inverse, grad_in_attn * (1.0 + scale_a))
    grad_tok_mod = jnp.concatenate(
        [
            grad_in_attn,
            grad_in_attn * normed,
            grad_mid * attn_out,
            grad_in_mlp,
            grad_in_mlp * normed_mlp,
            grad_out * mlp_out,
        ],
        axis=1,
    )
    grad_mod_part = lax.dot_general(
        onehot,
        grad_tok_mod,
        (((0,), (0,)), ((), ())),
        precision=lax.Precision.HIGHEST,
        preferred_element_type=jnp.float32,
    )
    grad_mod = lax.psum(grad_mod_part.astype(jnp.bfloat16), "shard")
    grad_cond_act = contract_cols(grad_mod, ada_weight)
    silu_back = jax.vjp(jax.nn.silu, cond)[1]
    grad_label = silu_back(grad_cond_act)[0]
    bins_count = lax.axis_size("bin")
    shard_count = lax.axis_size("shard")
    own_width = grad_mod.shape[1] // (bins_count * shard_count)
    mod_view = grad_mod.reshape(slots, bins_count, shard_count, own_width)
    own_columns = lax.dynamic_index_in_dim(
        mod_view, lax.axis_index("shard"), axis=2, keepdims=False
    )
    own_columns = own_columns.reshape(slots, bins_count * own_width)
    cond_rows = jnp.concatenate([cond_low, jnp.ones((slots, 1), jnp.bfloat16)], axis=1)
    ada_terms = contract_rows(cond_rows, own_columns).reshape(width + 1, bins_count, own_width)
    ada_sums = lax.psum_scatter(ada_terms, "bin", scatter_dimension=1, tiled=True)[:, 0, :]
    grad_ada_w = ada_sums[:width]
    grad_ada_b = ada_sums[width]
    weight_grads = (grad_qkv_w, grad_proj_w, grad_up_w, grad_down_w)
    shorter = (
        lax.psum_scatter(weight_grads[0], "bin", scatter_dimension=0, tiled=True),
        lax.psum_scatter(weight_grads[1], "bin", scatter_dimension=0, tiled=True),
        lax.psum_scatter(weight_grads[2], "bin", scatter_dimension=0, tiled=True),
        lax.psum_scatter(weight_grads[3], "bin", scatter_dimension=0, tiled=True),
    )
    grads_local = (
        lax.psum_scatter(
            shorter[0].astype(jnp.bfloat16), "shard", scatter_dimension=1, tiled=True
        ).astype(jnp.float32),
        lax.psum_scatter(
            shorter[1].astype(jnp.bfloat16), "shard", scatter_dimension=1, tiled=True
        ).astype(jnp.float32),
        lax.psum_scatter(
            shorter[2].astype(jnp.bfloat16), "shard", scatter_dimension=1, tiled=True
        ).astype(jnp.float32),
        lax.psum_scatter(
            shorter[3].astype(jnp.bfloat16), "shard", scatter_dimension=1, tiled=True
        ).astype(jnp.float32),
    )
    bias_sums = lax.psum((grad_qv_b, grad_proj_b, grad_up_b, grad_down_b), ("bin", "shard"))
    return (
        result,
        grad_input,
        grad_label,
        grad_ada_w,
        grad_ada_b,
        grads_local[0],
        bias_sums[0],
        grads_local[1],
        bias_sums[1],
        grads_local[2],
        bias_sums[2],
        grads_local[3],
        bias_sums[3],
    )


def solution(mesh):
    placed = (
        P(("bin", "shard"), None),
        P("bin", None),
        P("bin"),
        P("bin"),
        P(),
        P(),
        P("bin", "shard"),
        P(),
        P("bin", "shard"),
        P(),
        P("bin", "shard"),
        P(),
        P("bin", "shard"),
        P(),
        P("bin"),
        P(("bin", "shard"), None),
    )
    return jax.shard_map(
        per_device,
        mesh=mesh,
        in_specs=placed,
        out_specs=(
            P(("bin", "shard"), None),
            P(("bin", "shard"), None),
            P("bin", None),
            P(None, ("bin", "shard")),
            P(("bin", "shard")),
            P("bin", "shard"),
            P(),
            P("bin", "shard"),
            P(),
            P("bin", "shard"),
            P(),
            P("bin", "shard"),
            P(),
        ),
        check_vma=False,
    )
```

profile of v0, /device:TPU:0, one launch (start us, length us, event | category | flops | bytes accessed | tf_op | source)
XLA Modules:
  0.0 2135.6 jit_solution(2418818417426220248)
XLA Ops:
  61.3 47.6 %all-gather.37.cloned.1.call-done = bf16[1152,3456]{1,0:T(8,128)(2,1)} async-done(((bf16[144,3456]{1,0:T(8,128)(2,1)}), bf16[1152,3456]{1,0:T(8,128)(2,1)}) %all-gather.37.cloned.1.call-update) | async-done | bytes 7962640 | tf_op jit(solution)/shard_map/all_gather | solution.py:131
  150.4 36.1 %all-gather.45.cloned.1.call-done = bf16[576,1152]{0,1:T(8,128)(2,1)} async-done(((bf16[576,288]{0,1:T(8,128)(2,1)}), bf16[576,1152]{0,1:T(8,128)(2,1)}) %all-gather.45.cloned.1.call-update) | async-done | bytes 1327120 | tf_op jit(solution)/shard_map/all_gather | solution.py:128
  189.1 31.8 %all-gather = bf16[4,864,144]{1,2,0:T(8,128)(2,1)S(1)} all-gather(bf16[1,864,144]{1,2,0:T(8,128)(2,1)S(1)} %bitcast.272), channel_id=1, replica_groups=mesh['bin'=8,'shard'=4] {'shard'}, dimensions={0}, use_global_device_ids=true | all-gather | bytes 1244160 | tf_op jit(solution)/shard_map/all_gather | solution.py:125
  228.5 56.9 %all-gather.39.cloned.1.call-done = bf16[2048,1152]{1,0:T(8,128)(2,1)} async-done(((bf16[512,1152]{1,0:T(8,128)(2,1)}), bf16[2048,1152]{1,0:T(8,128)(2,1)}) %all-gather.39.cloned.1.call-update) | async-done | bytes 4718608 | tf_op jit(solution)/shard_map/all_gather | solution.py:150
  292.0 84.0 %all-gather.41.cloned.1.call-done = bf16[2048,1152]{1,0:T(8,128)(2,1)} async-done(((bf16[512,1152]{1,0:T(8,128)(2,1)}), bf16[2048,1152]{1,0:T(8,128)(2,1)}) %all-gather.41.cloned.1.call-update) | async-done | bytes 4718608 | tf_op jit(solution)/shard_map/all_gather | solution.py:149
  383.9 70.7 %while.40 = (s32[]{:T(128)}, bf16[4,512,4,72]{1,3,2,0:T(8,128)(2,1)}, f32[4,4,512]{2,1,0:T(4,128)}, bf16[4,2048,4,72]{1,3,2,0:T(8,128)(2,1)}, bf16[4,512,4,72]{1...) while((s32[]{:T(128)}, ...), condition=%wide.region_13.14_spmd.clone, body=%wide.region_10.13_spmd.clone.sunk | while | flops 1259337728 | bytes 57848412 | solution.py:76
  485.7 52.5 %all-gather.47.cloned.1.call-done = bf16[4608,1152]{1,0:T(8,128)(2,1)} async-done(((bf16[576,1152]{1,0:T(8,128)(2,1)}), bf16[4608,1152]{1,0:T(8,128)(2,1)}) %all-gather.47.cloned.1.call-update) | async-done | bytes 10616848 | tf_op jit(solution)/shard_map/all_gather | solution.py:134
  580.2 236.6 %while.41 = (s32[]{:T(128)}, bf16[4,512,4,72]{1,3,2,0:T(8,128)(2,1)}, bf16[4,2048,4,72]{1,3,2,0:T(8,128)(2,1)}, bf16[4,2048,4,72]{1,3,2,0:T(8,128)(2,1)}, bf16[4...) while((s32[]{:T(128)}, ...), condition=%wide.region_20.21_spmd.clone, body=%wide.region_18.20_spmd.clone.sunk | while | flops 3084597248 | bytes 190455024 | solution.py:110
  837.4 65.6 %reduce-scatter.20.cloned.1.call-done = bf16[512,1152]{0,1:T(8,128)(2,1)} async-done(((bf16[2048,1152]{0,1:T(8,128)(2,1)}), bf16[512,1152]{0,1:T(8,128)(2,1)}) %reduce-scatter.20.cloned.1.call-update) | async-done | bytes 1179664 | tf_op jit(solution)/shard_map/reduce_scatter | solution.py:268
  903.0 88.2 %reduce-scatter.22.cloned.1.call-done = bf16[512,1152]{0,1:T(8,128)(2,1)} async-done(((bf16[2048,1152]{0,1:T(8,128)(2,1)}), bf16[512,1152]{0,1:T(8,128)(2,1)}) %reduce-scatter.22.cloned.1.call-update) | async-done | bytes 1179664 | tf_op jit(solution)/shard_map/reduce_scatter | solution.py:271
  1092.6 30.0 %reduce-scatter.28.cloned.1.call-done = f32[144,1152]{1,0:T(8,128)} async-done(((f32[1152,1152]{1,0:T(8,128)}), f32[144,1152]{1,0:T(8,128)}) %reduce-scatter.28.cloned.1.call-update) | async-done | bytes 663568 | tf_op jit(solution)/shard_map/reduce_scatter | solution.py:328
  1135.1 24.7 %all-reduce.4.cloned.1.call-done = bf16[8,6912]{1,0:T(8,128)(2,1)} async-done(((bf16[8,6912]{1,0:T(8,128)(2,1)}), bf16[8,6912]{1,0:T(8,128)(2,1)}) %all-reduce.4.cloned.1.call-update) | async-done | bytes 110608 | tf_op jit(solution)/shard_map/psum | solution.py:308
  1167.9 82.8 %all-gather.23.cloned.1.call-done = bf16[2048,1152]{1,0:T(8,128)(2,1)} async-done(((bf16[512,1152]{1,0:T(8,128)(2,1)}), bf16[2048,1152]{1,0:T(8,128)(2,1)}) %all-gather.23.cloned.1.call-update) | async-done | bytes 4718608 | tf_op jit(solution)/shard_map/all_gather | solution.py:150
  1257.4 83.1 %all-gather.25.cloned.1.call-done = bf16[2048,1152]{1,0:T(8,128)(2,1)} async-done(((bf16[512,1152]{1,0:T(8,128)(2,1)}), bf16[2048,1152]{1,0:T(8,128)(2,1)}) %all-gather.25.cloned.1.call-update) | async-done | bytes 4718608 | tf_op jit(solution)/shard_map/all_gather | solution.py:149
  1347.2 132.8 %reduce-scatter.30.cloned.1.call-done = f32[144,4608]{1,0:T(8,128)} async-done(((f32[1152,4608]{1,0:T(8,128)}), f32[144,4608]{1,0:T(8,128)}) %reduce-scatter.30.cloned.1.call-update) | async-done | bytes 2654224 | tf_op jit(solution)/shard_map/reduce_scatter | solution.py:329
  1484.5 89.8 %while.39 = (s32[]{:T(128)}, bf16[4,512,4,72]{1,3,2,0:T(8,128)(2,1)S(1)}, bf16[4,2048,4,72]{1,3,2,0:T(8,128)(2,1)}, bf16[4,512,4,72]{1,3,2,0:T(8,128)(2,1)}, bf1...) while((s32[]{:T(128)}, ...), condition=%wide.region_5.6_spmd.clone, body=%wide.region_2.5_spmd.clone.sunk | while | flops 1234176000 | bytes 38924372 | solution.py:76
  1580.9 72.8 %reduce-scatter.32.cloned.1.call-done = f32[576,1152]{1,0:T(8,128)} async-done(((f32[4608,1152]{1,0:T(8,128)}), f32[576,1152]{1,0:T(8,128)}) %reduce-scatter.32.cloned.1.call-update) | async-done | bytes 2654224 | tf_op jit(solution)/shard_map/reduce_scatter | solution.py:330
  1659.6 59.8 %all-gather.35.cloned.1.call-done = bf16[4608,1152]{1,0:T(8,128)(2,1)} async-done(((bf16[576,1152]{1,0:T(8,128)(2,1)}), bf16[4608,1152]{1,0:T(8,128)(2,1)}) %all-gather.35.cloned.1.call-update) | async-done | bytes 10616848 | tf_op jit(solution)/shard_map/all_gather | solution.py:134
  1719.3 65.6 %all-gather.31.cloned.1.call-done = bf16[1152,4608]{1,0:T(8,128)(2,1)} async-done(((bf16[144,4608]{1,0:T(8,128)(2,1)}), bf16[1152,4608]{1,0:T(8,128)(2,1)}) %all-gather.31.cloned.1.call-update) | async-done | bytes 10616848 | tf_op jit(solution)/shard_map/all_gather | solution.py:133
  1811.7 111.4 %reduce-scatter.26.cloned.1.call-done = f32[144,3456]{1,0:T(8,128)} async-done(((f32[1152,3456]{1,0:T(8,128)}), f32[144,3456]{1,0:T(8,128)}) %reduce-scatter.26.cloned.1.call-update) | async-done | bytes 1990672 | tf_op jit(solution)/shard_map/reduce_scatter | solution.py:327
  1929.7 41.0 %all-reduce.1 = (f32[2304]{0:T(1024)}, f32[1152]{0:T(1024)}, f32[4608]{0:T(1024)}, f32[1152]{0:T(1024)}) all-reduce(f32[2304]{0:T(1024)S(1)} %pad_maximum_fusion.2, f32[1152]{0:T(1024)S(1)} %copy-done.53, f32[4608]{0:T(1024)S(1)} %copy-done.56, f32[1152]{0:T(1024)S(1)} %copy-done.52), channel_id=1, replica_groups=mesh['bin'=8,'shard'=4] {'bin','shard'}, use_global_device_ids=true, to_apply=%region_31.32 | all-reduce | flops 9216 | bytes 73728 | tf_op jit(solution)/shard_map/psum | solution.py:346
  2005.1 46.1 %reduce-scatter.38.cloned.1.call-done = bf16[1152,144]{1,0:T(8,128)(2,1)} async-done(((bf16[4608,144]{1,0:T(8,128)(2,1)}), bf16[1152,144]{1,0:T(8,128)(2,1)}) %reduce-scatter.38.cloned.1.call-update) | async-done | bytes 331792
  2053.3 33.3 %reduce-scatter.40.cloned.1.call-done = bf16[288,576]{1,0:T(8,128)(2,1)} async-done(((bf16[1152,576]{1,0:T(8,128)(2,1)}), bf16[288,576]{1,0:T(8,128)(2,1)}) %reduce-scatter.40.cloned.1.call-update) | async-done | bytes 331792
  2088.9 37.3 %reduce-scatter.34.cloned.1.call-done = bf16[864,144]{1,0:T(8,128)(2,1)} async-done(((bf16[3456,144]{1,0:T(8,128)(2,1)}), bf16[864,144]{1,0:T(8,128)(2,1)}) %reduce-scatter.34.cloned.1.call-update) | async-done | bytes 248848
  (405 shorter events, 835.0 us)
Async XLA Ops:
  57.6 227.7 %all-gather.39.cloned.1.call-start = ((), (), s32[]{:S(2)}) async-start(), calls=%async_computation.20 | async-start | bytes 5898240 | tf_op jit(solution)/shard_map/all_gather | solution.py:150
  119.2 256.8 %all-gather.41.cloned.1.call-start = ((), (), s32[]{:S(2)}) async-start(), calls=%async_computation.21 | async-start | bytes 5898240 | tf_op jit(solution)/shard_map/all_gather | solution.py:149
  119.8 334.8 %all-gather.43.cloned.1.call-start = ((), (), s32[]{:S(2)}) async-start(), calls=%async_computation.22 | async-start | bytes 2985984 | tf_op jit(solution)/shard_map/all_gather | solution.py:132
  142.0 330.6 %all-gather.51.cloned.1.call-start = ((), (), s32[]{:S(2)}) async-start(), calls=%async_computation.26 | async-start | bytes 11943936 | tf_op jit(solution)/shard_map/all_gather | solution.py:133
  150.3 387.8 %all-gather.47.cloned.1.call-start = ((), (), s32[]{:S(2)}) async-start(), calls=%async_computation.24 | async-start | bytes 11943936 | tf_op jit(solution)/shard_map/all_gather | solution.py:134
  189.1 636.6 %all-gather.21.cloned.1.call-start = ((), (), s32[]{:S(2)}) async-start(), calls=%async_computation.11 | async-start | bytes 8957952 | tf_op jit(solution)/shard_map/all_gather | solution.py:131
  223.0 680.0 %reduce-scatter.20.cloned.1.call-start = ((), (), s32[]{:S(2)}) async-start(), calls=%async_computation.27 | async-start | bytes 5898240 | tf_op jit(solution)/shard_map/reduce_scatter | solution.py:268
  817.5 271.4 %all-gather.33.cloned.1.call-start = ((), (), s32[]{:S(2)}) async-start(), calls=%async_computation.17 | async-start | bytes 1843200 | tf_op jit(solution)/shard_map/all_gather | solution.py:128
  818.1 273.8 %all-gather.29.cloned.1.call-start = ((), (), s32[]{:S(2)}) async-start(), calls=%async_computation.15 | async-start | bytes 1658880 | tf_op jit(solution)/shard_map/all_gather | solution.py:127
  818.8 303.8 %reduce-scatter.28.cloned.1.call-start = ((), (), s32[]{:S(2)}) async-start(), calls=%async_computation.32 | async-start | bytes 5971968 | tf_op jit(solution)/shard_map/reduce_scatter | solution.py:328
  825.6 334.2 %all-reduce.4.cloned.1.call-start = ((), (), s32[]{:S(2)}) async-start(), calls=%async_computation.29 | async-start | bytes 221184 | tf_op jit(solution)/shard_map/psum | solution.py:308
  1037.8 212.9 %all-gather.23.cloned.1.call-start = ((), (), s32[]{:S(2)}) async-start(), calls=%async_computation.12 | async-start | bytes 5898240 | tf_op jit(solution)/shard_map/all_gather | solution.py:150
  1041.7 298.8 %all-gather.25.cloned.1.call-start = ((), (), s32[]{:S(2)}) async-start(), calls=%async_computation.13 | async-start | bytes 5898240 | tf_op jit(solution)/shard_map/all_gather | solution.py:149
  1042.3 437.8 %reduce-scatter.30.cloned.1.call-start = ((), (), s32[]{:S(2)}) async-start(), calls=%async_computation.33 | async-start | bytes 23887872 | tf_op jit(solution)/shard_map/reduce_scatter | solution.py:329
  1054.6 519.7 %all-gather.27.cloned.1.call-start = ((), (), s32[]{:S(2)}) async-start(), calls=%async_computation.14 | async-start | bytes 2985984 | tf_op jit(solution)/shard_map/all_gather | solution.py:132
  1073.8 580.0 %reduce-scatter.32.cloned.1.call-start = ((), (), s32[]{:S(2)}) async-start(), calls=%async_computation.34 | async-start | bytes 23887872 | tf_op jit(solution)/shard_map/reduce_scatter | solution.py:330
  1088.8 630.5 %all-gather.35.cloned.1.call-start = ((), (), s32[]{:S(2)}) async-start(), calls=%async_computation.18 | async-start | bytes 11943936 | tf_op jit(solution)/shard_map/all_gather | solution.py:134
  1091.8 693.1 %all-gather.31.cloned.1.call-start = ((), (), s32[]{:S(2)}) async-start(), calls=%async_computation.16 | async-start | bytes 11943936 | tf_op jit(solution)/shard_map/all_gather | solution.py:133
  1092.6 717.4 %reduce-scatter.36.cloned.1.call-start = ((), (), s32[]{:S(2)}) async-start(), calls=%async_computation.36 | async-start | bytes 737280
  1124.8 798.3 %reduce-scatter.26.cloned.1.call-start = ((), (), s32[]{:S(2)}) async-start(), calls=%async_computation.31 | async-start | bytes 17915904 | tf_op jit(solution)/shard_map/reduce_scatter | solution.py:327
  1135.0 866.2 %reduce-scatter.24.cloned.1.call-start = ((), (), s32[]{:S(2)}) async-start(), calls=%async_computation.30 | async-start | bytes 9953280 | tf_op jit(solution)/shard_map/reduce_scatter | solution.py:322
  1166.4 884.8 %reduce-scatter.38.cloned.1.call-start = ((), (), s32[]{:S(2)}) async-start(), calls=%async_computation.37 | async-start | bytes 2949120
  1484.3 602.3 %reduce-scatter.40.cloned.1.call-start = ((), (), s32[]{:S(2)}) async-start(), calls=%async_computation.38 | async-start | bytes 1843200
  1659.3 467.0 %reduce-scatter.34.cloned.1.call-start = ((), (), s32[]{:S(2)}) async-start(), calls=%async_computation.35 | async-start | bytes 2211840
  (86 other events, 3208.7 us)
Sparse Core Ops, SparseCore 0:
  56.3 52.6 all-gather.36
  110.5 39.7 all-gather.48
  151.9 34.5 all-gather.44
  187.9 97.3 all-gather.38
  286.7 89.2 all-gather.40
  408.8 63.7 all-gather.50
  474.5 63.6 all-gather.46
  540.7 52.4 all-gather.20
  816.9 86.1 reduce-scatter.19
  905.3 85.7 reduce-scatter.21
  992.6 35.8 all-gather.32
  1066.6 55.9 reduce-scatter.27
  1125.4 34.3 all-reduce.3
  1161.2 89.3 all-gather.22
  1252.7 87.7 all-gather.24
  1344.0 136.0 reduce-scatter.29
  1516.1 137.5 reduce-scatter.31
  1655.6 63.6 all-gather.34
  1721.2 63.6 all-gather.30
  1813.5 109.6 reduce-scatter.25
  1926.7 74.5 reduce-scatter.23
  2003.4 47.6 reduce-scatter.37
  2053.3 33.2 reduce-scatter.39
  2089.0 37.2 reduce-scatter.33
  (4 shorter events, 113.8 us)
where the time goes:
time: 2150 us; the launch traced here: 2140 us
  waiting for transfers between devices  1250 us (58%)
  matrix products  511 us (24%)
  blocking collectives  135 us (6%)
  other arithmetic  134 us (6%)
  local copies, waits for them, and re-layouts  84.8 us (4%)
    all_gather x2, waiting for transfers between devices, forward_pass(): lax.all_gather(qkv_low[:, width:2 * width], 'shard', axis=0, tiled=True)  167 us
    all_gather x2, waiting for transfers between devices, forward_pass(): lax.all_gather(qkv_low[:, 2 * width:], 'shard', axis=0, tiled=True)  140 us
    reduce_scatter x1, waiting for transfers between devices, per_device(): lax.psum_scatter(weight_grads[2], 'bin', scatter_dimension=0, tiled=True)  133 us
    unnamed x32, waiting for transfers between devices  124 us
    all_gather x2, waiting for transfers between devices, collect_weights(): lax.all_gather(wider[3], 'bin', axis=0, tiled=True)  112 us
    reduce_scatter x1, waiting for transfers between devices, per_device(): lax.psum_scatter(weight_grads[0], 'bin', scatter_dimension=0, tiled=True)  111 us
    dot_general x8, matrix products, matmul(): return jnp.dot(left, right, preferred_element_type=jnp.float32)  89.3 us
    reduce_scatter x1, waiting for transfers between devices, per_device(): lax.psum_scatter(grad_values_all.astype(jnp.bfloat16), 'shard', scatter_d...  88.2 us
  transfers between devices with their start and end apart: 28, of which 23 were waited for; matrix products, arithmetic and copies ran while one was open for 33% of the time, Pallas kernels for 0%

commit v1 on v0

v1 whole, which is shorter than its diff:
```python
import functools
import math

import jax
import jax.numpy as jnp
from jax import lax
from jax.experimental import pallas as pl
from jax.experimental.pallas import tpu as pltpu
from jax.sharding import PartitionSpec as P

HEADS = 16
HEAD_DIM = 72
BLOCK = 256
LONG = 4
BF = jnp.bfloat16
F32 = jnp.float32


def time_embed(time_index, width):
    half_width = width // 2
    freqs = jnp.exp(-math.log(10000.0) * jnp.arange(half_width, dtype=jnp.float32) / half_width)
    angles = time_index.astype(jnp.float32)[:, None] * freqs[None, :]
    return jnp.concatenate([jnp.cos(angles), jnp.sin(angles)], axis=1)


def layer_norm(value):
    center = value - jnp.mean(value, axis=-1, keepdims=True)
    inverse = lax.rsqrt(jnp.mean(center * center, axis=-1, keepdims=True) + 1e-06)
    return (center * inverse, inverse)


def norm_back(normed, inverse, grad_normed):
    mean_grad = jnp.mean(grad_normed, axis=-1, keepdims=True)
    mean_cross = jnp.mean(grad_normed * normed, axis=-1, keepdims=True)
    return inverse * (grad_normed - mean_grad - normed * mean_cross)


def dot(left, right, dims):
    return lax.dot_general(left, right, (dims, ((), ())), preferred_element_type=F32)


def per_block(rows, value):
    tokens, width = value.shape
    return jnp.broadcast_to(rows[:, None, :], (rows.shape[0], BLOCK, width)).reshape(tokens, width)


def ring(value, axis, shift):
    size = lax.axis_size(axis)
    return lax.ppermute(value, axis, [(i, (i + shift) % size) for i in range(size)])


def hop(value, axis, shift):
    size = lax.axis_size(axis)
    pairs = [(i, i + shift) for i in range(size) if 0 <= i + shift < size]
    return lax.ppermute(value, axis, pairs)


def swap(value, mask):
    size = lax.axis_size("bin")
    return lax.ppermute(value, "bin", [(i, i ^ mask) for i in range(size)])


def spread(slab, masks):
    blocks = {0: slab}
    for mask in masks:
        for key in list(blocks):
            blocks[key ^ mask] = swap(blocks[key], mask)
    return blocks


def assemble_body(count, place_ref, *refs):
    sources, out_ref, scratch, sem_in, sem_out = (
        refs[:count], refs[count], refs[count + 1], refs[count + 2], refs[count + 3])
    bin_at, shard_at = place_ref[0], place_ref[1]
    depth = count // 2
    copies = []
    for colour in range(2):
        for key in range(depth):
            for half in range(2):
                part = 2 * colour + half
                row = jnp.bitwise_xor(bin_at, key)
                column = jnp.bitwise_and(shard_at + (4 - part), 3)
                index = part * depth + key
                copy = pltpu.make_async_copy(
                    sources[colour * depth + key].at[half], scratch.at[part, key], sem_in.at[index])
                copy.start()
                copies.append((copy, scratch.at[part, key], out_ref.at[column, row], index))
    outs = []
    for copy, source, target, index in copies:
        copy.wait()
        out = pltpu.make_async_copy(source, target, sem_out.at[index])
        out.start()
        outs.append(out)
    for out in outs:
        out.wait()


def gather_weight(piece, place):
    bins, shards = lax.axis_size("bin"), lax.axis_size("shard")
    rows, columns = piece.shape
    if bins != 8 or shards != 4 or rows % 16:
        full = lax.all_gather(piece, "bin", axis=0)
        return lax.all_gather(full, "shard", axis=0)
    parts = [piece]
    for _ in range(3):
        parts.append(ring(parts[-1], "shard", 1))
    first = spread(jnp.stack(parts[:2]), [2, 4, 1])
    second = spread(jnp.stack(parts[2:]), [4, 2, 1])
    sources = [first[k] for k in range(bins)] + [second[k] for k in range(bins)]
    size = 2 * rows * columns * 32
    return pl.pallas_call(
        functools.partial(assemble_body, len(sources)),
        out_shape=jax.ShapeDtypeStruct((shards, bins, rows, columns), BF),
        in_specs=[pl.BlockSpec(memory_space=pltpu.SMEM)]
        + [pl.BlockSpec(memory_space=pl.ANY)] * len(sources),
        out_specs=pl.BlockSpec(memory_space=pl.ANY),
        scratch_shapes=[
            pltpu.VMEM((shards, bins, rows, columns), BF),
            pltpu.SemaphoreType.DMA((shards * bins,)),
            pltpu.SemaphoreType.DMA((shards * bins,)),
        ],
        compiler_params=pltpu.CompilerParams(vmem_limit_bytes=24 * 2**20),
        cost_estimate=pl.CostEstimate(flops=0, bytes_accessed=2 * size, transcendentals=0),
        name="assemble",
    )(place, *sources)


def product_body(groups, by_rows, flip, colour, place_ref, left_ref, right_ref, *refs):
    step = pl.program_id(0)
    part = step if colour is None else (step + 1 if colour == 0 else (step * 3 + 3) % 4)
    if colour == 1:
        part = jnp.where(step == 0, 3, 0)
    shard_at = jnp.bitwise_and(place_ref[1] + (4 - part), 3)
    tall = left_ref.shape[0] // (groups * 2 * (4 if by_rows else 1))
    wide = right_ref.shape[0] // (1 if by_rows else 4)
    rows = []
    for offset in range(groups):
        owner = jnp.bitwise_xor(place_ref[0], 2 * offset + flip)
        owner = owner * 4 + shard_at if by_rows else owner
        rows.append(left_ref[pl.ds(pl.multiple_of(owner * tall, 16), tall), :])
    left = jnp.concatenate(rows, axis=0)
    if by_rows:
        right = right_ref[...]
    else:
        right = right_ref[pl.ds(pl.multiple_of(shard_at * wide, 16), wide), :]
    result = dot(left, right, ((1,), (1,))).reshape(groups, tall, wide)
    if colour is None:
        refs[0][:, 0] = result.astype(BF)
        return
    result = result + refs[0][:, 0].astype(F32)
    bit = 1 if colour == 0 else groups // 2
    sent = [o for o in range(groups) if o & bit]
    kept = [o for o in range(groups) if not o & bit]
    for at, offset in enumerate(sent):
        refs[1][at, 0] = result[offset].astype(BF)
    for at, offset in enumerate(kept):
        refs[2][at, 0] = result[offset].astype(BF)


def product(place, left, right, by_rows, colour, arrived=None):
    groups = lax.axis_size("bin") // 2
    tall = left.shape[0] // (groups * 2 * (4 if by_rows else 1))
    wide = right.shape[0] // (1 if by_rows else 4)
    steps = 4 if colour is None else 2
    whole = lambda step, place_ref: (0, 0)
    block = lambda n: pl.BlockSpec((n, 1, tall, wide), lambda step, place_ref: (0, step, 0, 0))
    specs = [pl.BlockSpec(left.shape, whole), pl.BlockSpec(right.shape, whole)]
    operands = [left, right]
    if colour is None:
        shapes = jax.ShapeDtypeStruct((groups, 4, tall, wide), BF)
        out_specs = block(groups)
    else:
        half = jax.ShapeDtypeStruct((groups // 2, 2, tall, wide), BF)
        shapes = (half, half)
        out_specs = (block(groups // 2), block(groups // 2))
        index = (lambda step, place_ref: (0, step + 1, 0, 0)) if colour == 0 else (
            lambda step, place_ref: (0, 3 - 3 * step, 0, 0))
        specs.append(pl.BlockSpec((groups, 1, tall, wide), index))
        operands.append(arrived)
    flops = 2 * groups * steps * tall * wide * left.shape[1]
    moved = 2 * (left.size + right.size + groups * steps * tall * wide * (1 if colour is None else 2))
    return pl.pallas_call(
        functools.partial(product_body, groups, by_rows, 1 if colour is None else 0, colour),
        out_shape=shapes,
        grid_spec=pltpu.PrefetchScalarGridSpec(
            num_scalar_prefetch=1, grid=(steps,), in_specs=specs, out_specs=out_specs),
        compiler_params=pltpu.CompilerParams(vmem_limit_bytes=48 * 2**20),
        cost_estimate=pl.CostEstimate(flops=flops, bytes_accessed=moved, transcendentals=0),
        name="gradient",
    )(place, *operands)


def wide_sum(*terms):
    total = terms[0].astype(F32)
    for term in terms[1:]:
        total = total + term.astype(F32)
    return total


def scatter_gradient(place, left, right, by_rows=False):
    bins, shards = lax.axis_size("bin"), lax.axis_size("shard")
    tall = left.shape[0] // bins // (4 if by_rows else 1)
    if bins != 8 or shards != 4 or tall % 16:
        full = dot(left, right, ((1,), (1,))).astype(BF)
        shorter = lax.psum_scatter(full, "bin", scatter_dimension=0, tiled=True)
        return lax.psum_scatter(shorter, "shard", scatter_dimension=1, tiled=True).astype(F32)
    arrived = swap(product(place, left, right, by_rows, None), 1)
    kept = []
    for colour, masks in ((0, (2, 4)), (1, (4, 2))):
        sent, held = product(place, left, right, by_rows, colour, arrived)
        came = swap(sent, masks[0])
        came_last = swap(wide_sum(held[1], came[1]).astype(BF), masks[1])
        kept.append((held[0], came[0], came_last))
    piece = lambda colour, at: wide_sum(*[term[at] for term in kept[colour]])
    moving = ring(piece(0, 0).astype(BF), "shard", 1)
    moving = ring((piece(0, 1) + moving).astype(BF), "shard", 1)
    moving = ring((piece(1, 0) + moving).astype(BF), "shard", 1)
    total = piece(1, 1) + moving
    if by_rows:
        return lax.all_to_all(
            total.astype(BF), "shard", split_axis=1, concat_axis=0, tiled=True).astype(F32)
    return total


def probabilities(keys, query):
    scores = dot(keys, query, ((0,), (0,))) * (1.0 / math.sqrt(HEAD_DIM))
    expo = jnp.exp(scores - jnp.max(scores, axis=0, keepdims=True))
    return expo, jnp.sum(expo, axis=0, keepdims=True)


def blocks_of(ref, slots, first):
    return jnp.concatenate(
        [ref[0, :, pl.ds(pl.multiple_of(s * BLOCK, BLOCK), BLOCK)] for s in slots], axis=1)


def each_image(plan_ref, at, work):
    single = plan_ref[at, 0] == 1

    @pl.when(single)
    def _():
        work([plan_ref[at, 1]])

    @pl.when(jnp.logical_not(single))
    def _():
        work([plan_ref[at, 1 + i] for i in range(LONG)])


def attend_body(plan_ref, query_ref, keys_ref, values_ref, out_ref):
    for at in range(query_ref.shape[2] // BLOCK):
        here = pl.ds(at * BLOCK, BLOCK)

        def work(slots):
            expo, total = probabilities(blocks_of(keys_ref, slots, 0), query_ref[0, :, here])
            probs = (expo / total).astype(BF)
            out = dot(blocks_of(values_ref, slots, 0), probs, ((1,), (0,)))
            out_ref[0, :, here] = out.astype(BF)

        each_image(plan_ref, at, work)


def attend_back_body(
    plan_ref, query_ref, keys_ref, values_ref, grad_ref, dq_ref, dk_ref, dv_ref, dk_sum, dv_sum
):
    dk_sum[...] = jnp.zeros_like(dk_sum)
    dv_sum[...] = jnp.zeros_like(dv_sum)
    scale = 1.0 / math.sqrt(HEAD_DIM)
    for at in range(query_ref.shape[2] // BLOCK):
        here = pl.ds(at * BLOCK, BLOCK)

        def work(slots):
            query = query_ref[0, :, here]
            grad = grad_ref[0, :, here]
            keys = blocks_of(keys_ref, slots, 0)
            expo, total = probabilities(keys, query)
            probs = expo / total
            grad_probs = dot(blocks_of(values_ref, slots, 0), grad, ((0,), (0,)))
            delta = jnp.sum(grad_probs * probs, axis=0, keepdims=True)
            grad_scores = (probs * (grad_probs - delta)).astype(BF)
            dq_ref[0, :, here] = (dot(keys, grad_scores, ((1,), (0,))) * scale).astype(BF)
            dk = dot(query, grad_scores, ((1,), (1,))) * scale
            dv = dot(grad, probs.astype(BF), ((1,), (1,)))
            for i, slot in enumerate(slots):
                there = pl.ds(pl.multiple_of(slot * BLOCK, BLOCK), BLOCK)
                dk_sum[:, there] += dk[:, i * BLOCK:(i + 1) * BLOCK]
                dv_sum[:, there] += dv[:, i * BLOCK:(i + 1) * BLOCK]

        each_image(plan_ref, at, work)
    dk_ref[0] = dk_sum[...].astype(BF)
    dv_ref[0] = dv_sum[...].astype(BF)


def head_spec(tokens, first=0):
    return pl.BlockSpec((1, HEAD_DIM, tokens), lambda head, plan_ref: (head + first, 0, 0))


def attend(plan, queries, keys_values):
    tokens, window = queries.shape[2], keys_values.shape[2]
    return pl.pallas_call(
        attend_body,
        out_shape=jax.ShapeDtypeStruct((HEADS, HEAD_DIM, tokens), BF),
        grid_spec=pltpu.PrefetchScalarGridSpec(
            num_scalar_prefetch=1,
            grid=(HEADS,),
            in_specs=[head_spec(tokens), head_spec(window), head_spec(window, HEADS)],
            out_specs=head_spec(tokens),
        ),
        compiler_params=pltpu.CompilerParams(vmem_limit_bytes=40 * 2**20),
        cost_estimate=pl.CostEstimate(
            flops=4 * HEADS * tokens * 1024 * 256, bytes_accessed=6 * 2**20, transcendentals=0),
        name="attend",
    )(plan, queries, keys_values, keys_values)


def attend_back(plan, queries, keys_values, grads):
    tokens, window = queries.shape[2], keys_values.shape[2]
    shape = lambda n: jax.ShapeDtypeStruct((HEADS, HEAD_DIM, n), BF)
    return pl.pallas_call(
        attend_back_body,
        out_shape=(shape(tokens), shape(window), shape(window)),
        grid_spec=pltpu.PrefetchScalarGridSpec(
            num_scalar_prefetch=1,
            grid=(HEADS,),
            in_specs=[
                head_spec(tokens), head_spec(window), head_spec(window, HEADS), head_spec(tokens)],
            out_specs=(head_spec(tokens), head_spec(window), head_spec(window)),
            scratch_shapes=[pltpu.VMEM((HEAD_DIM, window), F32), pltpu.VMEM((HEAD_DIM, window), F32)],
        ),
        compiler_params=pltpu.CompilerParams(vmem_limit_bytes=48 * 2**20),
        cost_estimate=pl.CostEstimate(
            flops=10 * HEADS * tokens * 1024 * 256, bytes_accessed=12 * 2**20, transcendentals=0),
        name="attend_back",
    )(plan, queries, keys_values, keys_values, grads)


def plan_of(block_segments, first, own_blocks, shards):
    at = lax.axis_index("shard")
    count = block_segments.shape[0]
    numbers = jnp.arange(count, dtype=jnp.int32)
    rows = []
    for i in range(own_blocks):
        mine = block_segments[first + i]
        same = block_segments == mine
        begin = jnp.argmax(same).astype(jnp.int32)
        size = jnp.sum(same.astype(jnp.int32))
        cells = [jnp.where(size == 1, 1, LONG)]
        for j in range(LONG):
            block = jnp.minimum(begin + j, count - 1)
            owner = block // own_blocks
            inside = block % own_blocks
            slot = jnp.where(
                owner == at, inside,
                jnp.where(owner == at - 1, own_blocks + inside,
                          jnp.where(owner == at + 1, 2 * own_blocks + inside, 3 * own_blocks)))
            cells.append(slot)
        rows.append(jnp.stack(cells))
    far = jnp.where(at < shards // 2, (at + 2) * own_blocks, (at - 2) * own_blocks + own_blocks - 1)
    window = [first + i for i in range(own_blocks)]
    window += [first - own_blocks + i for i in range(own_blocks)]
    window += [first + own_blocks + i for i in range(own_blocks)]
    window = jnp.clip(jnp.stack(window + [far]), 0, count - 1)
    return jnp.stack(rows).astype(jnp.int32), window


def per_device(
    block_input,
    label_embed,
    time_index,
    segment_ids,
    ada_weight,
    ada_bias,
    qkv_weight,
    qv_bias,
    proj_weight,
    proj_bias,
    up_weight,
    up_bias,
    down_weight,
    down_bias,
    bin_weight,
    out_cotangent,
):
    tokens, width = block_input.shape
    slots = label_embed.shape[0]
    bins, shards = lax.axis_size("bin"), lax.axis_size("shard")
    bin_at, shard_at = lax.axis_index("bin"), lax.axis_index("shard")
    place = jnp.stack([bin_at, shard_at]).astype(jnp.int32)
    own_blocks = tokens // BLOCK
    lower = shard_at < shards // 2

    from_left = hop(block_input, "shard", 1)
    from_right = hop(block_input, "shard", -1)
    edge = jnp.where(lower, block_input[tokens - BLOCK:], block_input[:BLOCK])
    across = ring(edge, "shard", 2)

    qkv_parts = gather_weight(qkv_weight, place)
    proj_parts = gather_weight(proj_weight, place)
    up_parts = gather_weight(up_weight, place)
    down_rows = lax.all_to_all(down_weight, "shard", split_axis=0, concat_axis=1, tiled=True)
    down_parts = gather_weight(down_rows, place)
    full = lambda parts: parts.transpose(1, 2, 0, 3).reshape(
        bins * parts.shape[2], shards * parts.shape[3])
    qkv_full, proj_full, up_full = full(qkv_parts), full(proj_parts), full(up_parts)
    down_full = down_parts.transpose(1, 0, 2, 3).reshape(4 * width, width)

    cond = label_embed + time_embed(time_index, width)
    cond_low = jax.nn.silu(cond).astype(BF)
    modul = dot(cond_low, ada_weight, ((1,), (0,))) + ada_bias
    block_segments = segment_ids[::BLOCK]
    first = shard_at * own_blocks
    plan, window_blocks = plan_of(block_segments, first, own_blocks, shards)
    picked = (block_segments[window_blocks][:, None] == jnp.arange(slots, dtype=jnp.int32)[None, :]).astype(F32)
    rows = jnp.dot(picked, modul, precision=lax.Precision.HIGHEST, preferred_element_type=F32)
    own_rows = jnp.split(rows[:own_blocks], 6, axis=1)
    shift_a, scale_a, gate_a, shift_m, scale_m, gate_m = [
        row.reshape(own_blocks, 1, width) for row in own_rows]
    window_shift = rows[:, None, :width]
    window_scale = rows[:, None, width:2 * width]

    stacked = jnp.concatenate([block_input, from_left, from_right, across], axis=0)
    span = stacked.shape[0] // BLOCK
    in_blocks = lambda value: value.reshape(value.shape[0] // BLOCK, BLOCK, value.shape[1])
    flat = lambda value: value.reshape(value.shape[0] * BLOCK, value.shape[2])
    window_normed = layer_norm(in_blocks(stacked).astype(F32))[0]
    window_in = flat((window_normed * (1.0 + window_scale) + window_shift).astype(BF))
    x = in_blocks(block_input).astype(F32)
    normed, inverse = layer_norm(x)
    attn_in = window_in[:tokens]
    query = (dot(qkv_full[:, :width], attn_in, ((0,), (1,))) + qv_bias[:width, None]).astype(BF)
    kv_bias = jnp.concatenate([jnp.zeros((width,), F32), qv_bias[width:]])
    key_value = (dot(qkv_full[:, width:], window_in, ((0,), (1,))) + kv_bias[:, None]).astype(BF)
    query = query.reshape(HEADS, HEAD_DIM, tokens)
    key_value = key_value.reshape(2 * HEADS, HEAD_DIM, span * BLOCK)
    heads = attend(plan, query, key_value).reshape(width, tokens)
    attn_out = in_blocks(dot(heads, proj_full, ((0,), (0,))) + proj_bias)
    middle = x + gate_a * attn_out
    normed_mlp, inverse_mlp = layer_norm(middle)
    mlp_in = flat((normed_mlp * (1.0 + scale_m) + shift_m).astype(BF))
    pre_act = dot(mlp_in, up_full, ((1,), (0,))) + up_bias
    act_low = jax.nn.gelu(pre_act, approximate=True).astype(BF)
    mlp_out = in_blocks(dot(act_low, down_full, ((1,), (0,))) + down_bias)
    result = middle + gate_m * mlp_out

    grad_out = in_blocks(out_cotangent).astype(F32) * bin_weight[0]
    grad_mlp = flat((grad_out * gate_m).astype(BF))
    grad_down = scatter_gradient(place, act_low.T, grad_mlp.T, by_rows=True)
    grad_down_b = jnp.sum(grad_mlp.astype(F32), axis=0)
    grad_act = dot(grad_mlp, down_full, ((1,), (1,)))
    gelu_back = jax.vjp(lambda value: jax.nn.gelu(value, approximate=True), pre_act)[1]
    grad_pre = gelu_back(grad_act)[0].astype(BF)
    grad_up = scatter_gradient(place, mlp_in.T, grad_pre.T)
    grad_up_b = jnp.sum(grad_pre.astype(F32), axis=0)
    grad_in_mlp = in_blocks(dot(grad_pre, up_full, ((1,), (1,))))
    grad_mid = grad_out + norm_back(normed_mlp, inverse_mlp, grad_in_mlp * (1.0 + scale_m))
    grad_attn = flat((grad_mid * gate_a).astype(BF))
    grad_proj = scatter_gradient(place, heads, grad_attn.T)
    grad_proj_b = jnp.sum(grad_attn.astype(F32), axis=0)
    grad_heads = dot(proj_full, grad_attn, ((1,), (1,))).astype(BF).reshape(HEADS, HEAD_DIM, tokens)
    dq, dk, dv = attend_back(plan, query, key_value, grad_heads)
    rest = span * BLOCK - tokens
    dq = dq.reshape(width, tokens)
    grad_kv = jnp.concatenate([dk.reshape(width, -1), dv.reshape(width, -1)], axis=0)
    grad_qkv = jnp.concatenate(
        [jnp.pad(dq, ((0, 0), (0, rest))), grad_kv], axis=0)
    away = dot(grad_kv[:, tokens:], qkv_full[:, width:], ((0,), (1,))).astype(BF)
    home = dot(grad_qkv[:, :tokens], qkv_full, ((0,), (1,)))
    back_left = hop(away[:tokens], "shard", -1)
    back_right = hop(away[tokens:2 * tokens], "shard", 1)
    back_edge = ring(away[2 * tokens:], "shard", 2).astype(F32)
    none = jnp.zeros((tokens - BLOCK, width), F32)
    back_edge = jnp.where(
        lower, jnp.concatenate([none, back_edge]), jnp.concatenate([back_edge, none]))
    grad_in_attn = in_blocks(home + back_left.astype(F32) + back_right.astype(F32) + back_edge)
    grad_qkv_w = scatter_gradient(place, window_in.T, grad_qkv)
    grad_qv_b = jnp.concatenate(
        [jnp.sum(dq.astype(F32), axis=1), jnp.sum(grad_kv[width:].astype(F32), axis=1)])
    grad_input = grad_mid + norm_back(normed, inverse, grad_in_attn * (1.0 + scale_a))

    sums = jnp.concatenate(
        [
            jnp.sum(term, axis=1)
            for term in (
                grad_in_attn,
                grad_in_attn * normed,
                grad_mid * attn_out,
                grad_in_mlp,
                grad_in_mlp * normed_mlp,
                grad_out * mlp_out,
            )
        ],
        axis=1,
    )
    grad_mod_part = lax.dot_general(
        picked[:own_blocks], sums, (((0,), (0,)), ((), ())),
        precision=lax.Precision.HIGHEST, preferred_element_type=F32)
    grad_mod = lax.psum(grad_mod_part, "shard").astype(BF)
    grad_cond_act = dot(grad_mod, ada_weight, ((1,), (1,)))
    grad_label = jax.vjp(jax.nn.silu, cond)[1](grad_cond_act)[0]
    own_width = grad_mod.shape[1] // (bins * shards)
    mod_view = grad_mod.reshape(slots, bins, shards, own_width)
    columns = lax.dynamic_index_in_dim(mod_view, shard_at, axis=2, keepdims=False)
    columns = lax.all_gather(columns, "bin", axis=0)
    columns = lax.dynamic_index_in_dim(columns, bin_at, axis=2, keepdims=False)
    columns = columns.reshape(bins * slots, own_width)
    cond_all = lax.all_gather(cond_low, "bin", axis=0, tiled=True)
    grad_ada_w = dot(cond_all, columns, ((0,), (0,)))
    grad_ada_b = jnp.sum(columns.astype(F32), axis=0)
    bias_sums = lax.psum((grad_qv_b, grad_proj_b, grad_up_b, grad_down_b), ("bin", "shard"))
    return (
        flat(result),
        flat(grad_input),
        grad_label,
        grad_ada_w,
        grad_ada_b,
        grad_qkv_w,
        bias_sums[0],
        grad_proj,
        bias_sums[1],
        grad_up,
        bias_sums[2],
        grad_down,
        bias_sums[3],
    )


def solution(mesh):
    placed = (
        P(("bin", "shard"), None),
        P("bin", None),
        P("bin"),
        P("bin"),
        P(),
        P(),
        P("bin", "shard"),
        P(),
        P("bin", "shard"),
        P(),
        P("bin", "shard"),
        P(),
        P("bin", "shard"),
        P(),
        P("bin"),
        P(("bin", "shard"), None),
    )
    return jax.shard_map(
        per_device,
        mesh=mesh,
        in_specs=placed,
        out_specs=(
            P(("bin", "shard"), None),
            P(("bin", "shard"), None),
            P("bin", None),
            P(None, ("bin", "shard")),
            P(("bin", "shard")),
            P("bin", "shard"),
            P(),
            P("bin", "shard"),
            P(),
            P("bin", "shard"),
            P(),
            P("bin", "shard"),
            P(),
        ),
        check_vma=False,
    )
```

time: 2150 us -> 1070 us (0.50)
  waiting for transfers between devices: 1250 us -> 170 us
  matrix products: 511 us -> 132 us
  Pallas kernels: 0 us -> 161 us
  starting transfers between devices: 1.39 us -> 142 us
  local copies, waits for them, and re-layouts: 84.8 us -> 222 us
  blocking collectives: 135 us -> 106 us
  other arithmetic: 134 us -> 107 us
    all_gather x16 -> x0, waiting for transfers between devices: 583 us -> none  [the longest x2 167 us: forward_pass(): lax.all_gather(qkv_low[:, width:2 * width], 'shard', axis=0, tiled=True)]
    reduce_scatter x7 -> x0, waiting for transfers between devices: 521 us -> none  [the longest x1 133 us: per_device(): lax.psum_scatter(weight_grads[2], 'bin', scatter_dimension=0, tiled=True)]
    dot_general x52 -> x15, matrix products: 463 us -> 132 us  [the longest x13 131 us: dot(): lax.dot_general(left, right, (dims, ((), ())), preferred_element_type=F32)]
    ppermute x0 -> x106, waiting for transfers between devices: none -> 164 us  [the longest x76 90.5 us: swap(): return lax.ppermute(value, 'bin', [(i, i ^ mask) for i in range(size)])]
    pallas_call x0 -> x18, Pallas kernels: none -> 161 us  [the longest x12 80.1 us: product(): pl.pallas_call(functools.partial(product_body, groups, by_rows, 1 if colo...]
    ppermute x0 -> x106, starting transfers between devices: none -> 134 us  [the longest x76 74.3 us: swap(): return lax.ppermute(value, 'bin', [(i, i ^ mask) for i in range(size)])]
    unnamed x32 -> x0, waiting for transfers between devices: 124 us -> none
    all_gather x4 -> x2, blocking collectives: 93.7 us -> 20.7 us  [the longest x1 10.4 us: per_device(): cond_all = lax.all_gather(cond_low, 'bin', axis=0, tiled=True)]
  transfers between devices with their start and end apart: 28 -> 108, of which waited for: 23 -> 25; matrix products, arithmetic and copies ran while one was open for 33% -> 32% of each run, Pallas kernels for 0% -> 12%
where the time goes in v1:
time: 1070 us; the launch traced here: 1050 us
  local copies, waits for them, and re-layouts  222 us (21%)
  waiting for transfers between devices  170 us (16%)
  Pallas kernels  161 us (15%)
  starting transfers between devices  142 us (13%)
  matrix products  132 us (12%)
  other arithmetic  107 us (10%)
  blocking collectives  106 us (10%)
    dot_general x13, matrix products, dot(): lax.dot_general(left, right, (dims, ((), ())), preferred_element_type=F32)  131 us
    ppermute x76, waiting for transfers between devices, swap(): return lax.ppermute(value, 'bin', [(i, i ^ mask) for i in range(size)])  90.5 us
    pallas_call x12, Pallas kernels, product(): pl.pallas_call(functools.partial(product_body, groups, by_rows, 1 if colo...  80.1 us
    ppermute x76, starting transfers between devices, swap(): return lax.ppermute(value, 'bin', [(i, i ^ mask) for i in range(size)])  74.3 us
    ppermute x26, waiting for transfers between devices, ring(): lax.ppermute(value, axis, [(i, (i + shift) % size) for i in range(size)])  73.4 us
    psum x1, blocking collectives, per_device(): lax.psum((grad_qv_b, grad_proj_b, grad_up_b, grad_down_b), ('bin', 'shard'))  63 us
    pallas_call x4, Pallas kernels, gather_weight(): pl.pallas_call(functools.partial(assemble_body, len(sources)), out_shape=...  39.5 us
    ppermute x4, starting transfers between devices, hop(): return lax.ppermute(value, axis, pairs)  36.5 us
  transfers between devices with their start and end apart: 108, of which 25 were waited for; matrix products, arithmetic and copies ran while one was open for 32% of the time, Pallas kernels for 12%

profile of v1, /device:TPU:0, one launch (start us, length us, event | category | flops | bytes accessed | tf_op | source)
XLA Modules:
  0.0 1050.2 jit_solution(14891465805120987820)
XLA Ops:
  124.6 10.4 all_gather.9
  181.4 17.7 %collective-permute-done.46 = bf16[144,1152]{1,0:T(8,128)(2,1)S(1)} collective-permute-done((bf16[144,1152]{1,0:T(8,128)(2,1)}, bf16[144,1152]{1,0:T(8,128)(2,1)S(1)}, u32[]{:S(2)}, u32[]{:S(2)}) %collective-permute-start.46) | collective-permute-done | bytes 331808 | tf_op jit(solution)/shard_map/ppermute | solution.py:49
  263.3 17.5 %assemble.4 = bf16[4,8,144,864]{3,2,1,0:T(8,128)(2,1)S(1)} custom-call(s32[2]{0:T(128)S(1)} %pad_add_fusion.1.place_ref, bf16[2,144,864]{2,1,0:T(8,128)(2,1)S(1)} %pad_maximum_fusion.7.refs_0_, bf16[2,144,864]{2,1,0:T(8,128)(2,1)S(1)} %copy-done.25, bf16[2,144,864]{2,1,0:T(8,128)(2,1)S(1)} %copy-done.23, bf16[2,144,864]{2,1,0:T(8,128)(2,1)S(1)} %copy-done.29, ...), custom_call_target="tpu_custom_call" | custom-call | bytes 15925248 | tf_op jit(solution)/shard_map/assemble/pallas_call | solution.py:111
  288.1 14.5 %reshape.563 = bf16[1152,3456]{1,0:T(8,128)(2,1)} reshape(bf16[8,144,4,864]{3,2,1,0:T(4,128)(2,1)} %copy.151) | data formatting | bytes 15925248 | tf_op jit(solution)/shard_map/reshape | solution.py:400
  304.9 14.7 %add_convert_fusion = bf16[2304,1792]{1,0:T(8,128)(2,1)S(1)} fusion(bf16[1792,1152]{0,1:T(8,128)(2,1)} %add_convert_fusion.1, f32[2304]{0:T(1024)S(1)} %concatenate.37, bf16[1152,3456]{1,0:T(8,128)(2,1)} %reshape.563), kind=kOutput, calls=%fused_computation.3 | convolution fusion | flops 9520939008 | bytes 17703936 | tf_op jit(solution)/shard_map/dot_general | solution.py:39
  325.0 16.9 %attend.1 = bf16[16,72,512]{2,1,0:T(8,128)(2,1)S(1)} custom-call(s32[2,5]{1,0:T(2,128)S(1)} %pad_add_fusion.plan_ref, bf16[16,72,512]{2,1,0:T(8,128)(2,1)S(1)} %bitcast.299, bf16[32,72,1792]{2,1,0:T(8,128)(2,1)S(1)} %bitcast.295, bf16[32,72,1792]{2,1,0:T(8,128)(2,1)S(1)} %bitcast.296), custom_call_target="tpu_custom_call" | custom-call | flops 8589934592 | bytes 6291456 | tf_op jit(solution)/shard_map/attend/pallas_call | solution.py:298
  379.2 16.9 %copy.165 = bf16[8,144,4,1152]{3,2,1,0:T(4,128)(2,1)S(1)} copy(bf16[8,144,4,1152]{3,1,0,2:T(8,128)(2,1)S(1)} %bitcast.274) | data formatting | bytes 21233664 | tf_op jit(solution)/shard_map/transpose | solution.py:400
  406.0 12.0 %convolution_add_fusion.1 = f32[512,4608]{0,1:T(8,128)} fusion(bf16[512,1152]{0,1:T(8,128)(2,1)S(1)} %add_convert_fusion.2, bf16[1152,4608]{1,0:T(8,128)(2,1)} %bitcast.308, f32[4608]{0:T(1024)S(1)} %copy-done.86), kind=kOutput, calls=%fused_computation.37 | convolution fusion | flops 5438177280 | bytes 21252096 | tf_op jit(solution)/shard_map/dot_general | solution.py:39
  418.0 15.5 %reshape.609 = bf16[1152,4608,1]{1,0,2:T(8,128)(2,1)} reshape(bf16[8,144,4,1152]{3,2,1,0:T(4,128)(2,1)} %copy-done.43) | data formatting | bytes 21233664 | tf_op jit(solution)/shard_map/reshape | solution.py:400
  445.1 18.5 %convert_reduce_fusion.3 = (f32[1152]{0:T(1024)}, bf16[512,1152]{0,1:T(8,128)(2,1)S(1)}, f32[512,1152]{0,1:T(8,128)}, f32[512,1152]{0,1:T(8,128)}, f32[512,1152]{0,1:T(8,128)}) fusion(f32[512,1152]{0,1:T(8,128)} %bitcast.328, f32[]{:T(128)} %bitcast.273, bf16[512,1152]{0,1:T(8,128)(2,1)S(1)} %copy-done.56, f32[512,1152]{0,1:T(8,128)} %get-tuple-element.130, ...), kind=kOutput, calls=%fused_computation.62 | convolution fusion | flops 5462359040 | bytes 34219012 | tf_op jit(solution)/shard_map/dot_general | solution.py:39
  463.6 20.1 %convert_reduce_fusion = (f32[4608]{0:T(1024)}, bf16[512,4608]{0,1:T(8,128)(2,1)}, f32[512,4608]{0,1:T(8,128)}) fusion(f32[512,4608]{0,1:T(8,128)} %convolution_add_fusion.1, bf16[4608,1152]{1,0:T(8,128)(2,1)} %bitcast.310, bf16[512,1152]{0,1:T(8,128)(2,1)S(1)} %get-tuple-element.120), kind=kOutput, calls=%fused_computation.31 | convolution fusion | flops 5487717888 | bytes 35407872 | tf_op jit(solution)/shard_map/dot_general | solution.py:39
  499.3 14.5 %multiply_reduce_fusion.2 = (f32[2,1152]{1,0:T(2,128)}, f32[2,256]{1,0:T(2,128)S(1)}, f32[2,256]{1,0:T(2,128)S(1)}, f32[2,1152]{1,0:T(2,128)}, f32[2,256,1152]{2,1,0:T(8,128)S(1)}, /*index=5*/f32[2,256,1152]{2,1,0:T(8,128)}) fusion(f32[2,1152]{1,0:T(2,128)S(1)} %copy-done.69, f32[2,256]{1,0:T(2,128)S(1)} %rsqrt.39, f32[2,256]{1,0:T(2,128)S(1)} %div.142, ...), kind=kOutput, calls=%fused_computation.66 | convolution fusion | flops 5442300928 | bytes 24817664 | tf_op jit(solution)/shard_map/dot_general | solution.py:39
  524.3 24.5 %attend_back.1 = (bf16[16,72,512]{2,1,0:T(8,128)(2,1)S(1)}, bf16[16,72,1792]{2,1,0:T(8,128)(2,1)}, bf16[16,72,1792]{2,1,0:T(8,128)(2,1)}) custom-call(s32[2,5]{1,0:T(2,128)S(1)} %pad_add_fusion.plan_ref, bf16[16,72,512]{2,1,0:T(8,128)(2,1)S(1)} %bitcast.300, bf16[32,72,1792]{2,1,0:T(8,128)(2,1)} %bitcast.297, bf16[32,72,1792]{2,1,0:T(8,128)(2,1)} %bitcast.298, ...), custom_call_target="tpu_custom_call" | custom-call | flops 21474836480 | bytes 12582912 | tf_op jit(solution)/shard_map/attend_back/pallas_call | solution.py:317
  580.6 14.5 %collective-permute-start.98 = (bf16[4,4,144,1152]{3,2,1,0:T(8,128)(2,1)}, bf16[4,4,144,1152]{3,2,1,0:T(8,128)(2,1)}, u32[]{:S(2)}, u32[]{:S(2)}) collective-permute-start(bf16[4,4,144,1152]{3,2,1,0:T(8,128)(2,1)} %gradient.21), channel_id=1, source_target_pairs={{0,4},{4,0},{8,12},{12,8},{16,20},{20,16},{24,28},{28,24},{1,5},{5... | collective-permute-start | bytes 15925256 | tf_op jit(solution)/shard_map/ppermute | solution.py:60
  602.5 10.4 fusion.2.right_ref
  618.1 31.6 %collective-permute-start.72 = (bf16[512,1152]{0,1:T(8,128)(2,1)}, bf16[512,1152]{0,1:T(8,128)(2,1)}, u32[]{:S(2)}, u32[]{:S(2)}) collective-permute-start(bf16[512,1152]{0,1:T(8,128)(2,1)} %get-tuple-element.134), channel_id=1, source_target_pairs={{0,1},{1,2},{2,3},{4,5},{5,6},{6,7},{8,9},{9,10},{10,11},{12,13},{... | collective-permute-start | bytes 3538952 | tf_op jit(solution)/shard_map/ppermute | solution.py:55
  660.7 63.0 %all-reduce.4 = (f32[2304]{0:T(1024)}, f32[1152]{0:T(1024)}, f32[4608]{0:T(1024)}, f32[1152]{0:T(1024)}) all-reduce(f32[2304]{0:T(1024)S(1)} %pad_maximum_fusion.11, f32[1152]{0:T(1024)} %get-tuple-element.123, f32[4608]{0:T(1024)} %get-tuple-element.121, ...), channel_id=1, replica_groups=mesh['bin'=8,'shard'=4] {'bin','shard'}, use_global_device_ids=true, to_apply=%region_24.25 | all-reduce | flops 9216 | bytes 73728 | tf_op jit(solution)/shard_map/psum | solution.py:507
  727.4 17.0 %gradient.12 = bf16[4,4,144,864]{3,2,1,0:T(8,128)(2,1)} custom-call(s32[2]{0:T(128)S(1)} %pad_add_fusion.1.place_ref, bf16[1152,1792]{1,0:T(8,128)(2,1)} %bitcast.276, bf16[3456,1792]{1,0:T(8,128)(2,1)} %fusion.2.right_ref), custom_call_target="tpu_custom_call" | custom-call | flops 7134511104 | bytes 20496384 | tf_op jit(solution)/shard_map/gradient/pallas_call | solution.py:182
  746.1 12.2 %multiply_reduce_fusion.10 = (f32[512]{0:T(512)}, f32[512]{0:T(512)}, f32[512,1152]{0,1:T(8,128)}) fusion(f32[512,1152]{0,1:T(8,128)S(1)} %copy-done.52, f32[512]{0:T(512)S(1)} %copy-done.83, f32[512]{0:T(512)S(1)} %copy-done.81, bf16[512,1152]{0,1:T(8,128)(2,1)S(1)} %copy-done.47, f32[256,1152]{0,1:T(8,128)S(1)} %convert_element_type.565, pred[]{:T(512)S(6)} %lt.65, ...), kind=kOutput, calls=%fused_computation.89 | convolution fusion | flops 4084530176 | bytes 20946944 | tf_op jit(solution)/shard_map/dot_general | solution.py:39
  785.4 22.5 %all-reduce.6 = bf16[8,6912]{1,0:T(8,128)(2,1)} all-reduce(f32[8,6912]{1,0:T(8,128)} %fusion.81), channel_id=1, replica_groups=mesh['bin'=8,'shard'=4] {'shard'}, use_global_device_ids=true, to_apply=%region_20.21 | all-reduce | flops 55296 | bytes 331776 | tf_op jit(solution)/shard_map/psum | solution.py:495
  821.9 10.4 fusion.77
  858.3 10.3 gradient.13
  886.1 23.3 %collective-permute-done.78 = bf16[2,144,864]{2,1,0:T(8,128)(2,1)S(1)} collective-permute-done((bf16[2,144,864]{2,1,0:T(8,128)(2,1)S(1)}, bf16[2,144,864]{2,1,0:T(8,128)(2,1)S(1)}, u32[]{:S(2)}, u32[]{:S(2)}) %collective-permute-start.78) | collective-permute-done | bytes 497696 | tf_op jit(solution)/shard_map/ppermute | solution.py:60
  959.1 25.9 %collective-permute-done.93 = bf16[2,2,144,1152]{3,2,1,0:T(8,128)(2,1)S(1)} collective-permute-done((bf16[2,2,144,1152]{3,2,1,0:T(8,128)(2,1)S(1)}, bf16[2,2,144,1152]{3,2,1,0:T(8,128)(2,1)S(1)}, u32[]{:S(2)}, u32[]{:S(2)}) %collective-permute-start.93) | collective-permute-done | bytes 1327136 | tf_op jit(solution)/shard_map/ppermute | solution.py:60
  (564 shorter events, 585.5 us)
Async XLA Ops:
  0.6 44.5 %collective-permute-start = (bf16[144,864]{1,0:T(8,128)(2,1)}, bf16[144,864]{1,0:T(8,128)(2,1)S(1)}, u32[]{:S(2)}, u32[]{:S(2)}) collective-permute-start(bf16[144,864]{1,0:T(8,128)(2,1)} %param.22), channel_id=1, source_target_pairs={{0,1},{1,2},{2,3},{3,0},{4,5},{5,6},{6,7},{7,4},{8,9},{9,10},{10,1... | collective-permute-start | bytes 746504 | tf_op jit(solution)/shard_map/ppermute | solution.py:49
  5.3 40.4 %collective-permute-start.37 = (bf16[144,1152]{1,0:T(8,128)(2,1)}, bf16[144,1152]{1,0:T(8,128)(2,1)}, u32[]{:S(2)}, u32[]{:S(2)}) collective-permute-start(bf16[144,1152]{1,0:T(8,128)(2,1)} %param.26), channel_id=1, source_target_pairs={{0,1},{1,2},{2,3},{3,0},{4,5},{5,6},{6,7},{7,4},{8,9},{9,10},{10,1... | collective-permute-start | bytes 995336 | tf_op jit(solution)/shard_map/ppermute | solution.py:49
  8.8 129.7 %all-to-all-start = ((bf16[4,144,288]{2,1,0:T(8,128)(2,1)}), bf16[4,144,288]{2,1,0:T(8,128)(2,1)}, u32[]{:S(2)}, u32[]{:S(2)}) async-start(bf16[4,144,288]{2,1,0:T(8,128)(2,1)} %bitcast.48), calls=%async_computation | async-start | bytes 884736 | tf_op jit(solution)/shard_map/all_to_all | solution.py:398
  62.3 149.4 %collective-permute-start.17 = (bf16[512,1152]{0,1:T(8,128)(2,1)}, bf16[512,1152]{0,1:T(8,128)(2,1)}, u32[]{:S(2)}, u32[]{:S(2)}) collective-permute-start(bf16[512,1152]{0,1:T(8,128)(2,1)} %copy-done.44), channel_id=1, source_target_pairs={{0,1},{1,2},{2,3},{4,5},{5,6},{6,7},{8,9},{9,10},{10,11},{12,13},{... | collective-permute-start | bytes 3538952 | tf_op jit(solution)/shard_map/ppermute | solution.py:55
  64.5 148.4 %collective-permute-start.18 = (bf16[512,1152]{0,1:T(8,128)(2,1)}, bf16[512,1152]{0,1:T(8,128)(2,1)}, u32[]{:S(2)}, u32[]{:S(2)}) collective-permute-start(bf16[512,1152]{0,1:T(8,128)(2,1)} %copy-done.44), channel_id=1, source_target_pairs={{1,0},{2,1},{3,2},{5,4},{6,5},{7,6},{9,8},{10,9},{11,10},{13,12},{... | collective-permute-start | bytes 3538952 | tf_op jit(solution)/shard_map/ppermute | solution.py:55
  65.8 69.2 %collective-permute-start.32 = (bf16[2,144,288]{2,1,0:T(8,128)(2,1)S(1)}, bf16[2,144,288]{2,1,0:T(8,128)(2,1)S(1)}, u32[]{:S(2)}, u32[]{:S(2)}) collective-permute-start(bf16[2,144,288]{2,1,0:T(8,128)(2,1)S(1)} %collective-permute-done.31.refs_10_), channel_id=1, source_target_pairs={{0,4},{4,0},{8,12},{12,8},{16,20},{20,16},{24,28},{28,24},{1,5},{5... | collective-permute-start | bytes 497672 | tf_op jit(solution)/shard_map/ppermute | solution.py:60
  66.4 76.2 %collective-permute-start.27 = (bf16[2,144,288]{2,1,0:T(8,128)(2,1)S(1)}, bf16[2,144,288]{2,1,0:T(8,128)(2,1)S(1)}, u32[]{:S(2)}, u32[]{:S(2)}) collective-permute-start(bf16[2,144,288]{2,1,0:T(8,128)(2,1)S(1)} %collective-permute-done.26.refs_6_), channel_id=1, source_target_pairs={{0,4},{4,0},{8,12},{12,8},{16,20},{20,16},{24,28},{28,24},{1,5},{5... | collective-permute-start | bytes 497672 | tf_op jit(solution)/shard_map/ppermute | solution.py:60
  66.5 77.8 %collective-permute-start.36 = (bf16[2,144,288]{2,1,0:T(8,128)(2,1)S(1)}, bf16[2,144,288]{2,1,0:T(8,128)(2,1)}, u32[]{:S(2)}, u32[]{:S(2)}) collective-permute-start(bf16[2,144,288]{2,1,0:T(8,128)(2,1)S(1)} %collective-permute-done.35.refs_14_), channel_id=1, source_target_pairs={{0,4},{4,0},{8,12},{12,8},{16,20},{20,16},{24,28},{28,24},{1,5},{5... | collective-permute-start | bytes 497672 | tf_op jit(solution)/shard_map/ppermute | solution.py:60
  135.0 41.2 %collective-permute-start.45 = (bf16[144,1152]{1,0:T(8,128)(2,1)}, bf16[144,1152]{1,0:T(8,128)(2,1)}, u32[]{:S(2)}, u32[]{:S(2)}) collective-permute-start(bf16[144,1152]{1,0:T(8,128)(2,1)} %collective-permute-done.37), channel_id=1, source_target_pairs={{0,1},{1,2},{2,3},{3,0},{4,5},{5,6},{6,7},{7,4},{8,9},{9,10},{10,1... | collective-permute-start | bytes 995336 | tf_op jit(solution)/shard_map/ppermute | solution.py:49
  253.6 49.1 %collective-permute-start.39 = (bf16[2,144,1152]{2,1,0:T(8,128)(2,1)S(1)}, bf16[2,144,1152]{2,1,0:T(8,128)(2,1)}, u32[]{:S(2)}, u32[]{:S(2)}) collective-permute-start(bf16[2,144,1152]{2,1,0:T(8,128)(2,1)S(1)} %pad_maximum_fusion.3.refs_0_), channel_id=1, source_target_pairs={{0,8},{4,12},{8,0},{12,4},{16,24},{20,28},{24,16},{28,20},{1,9},{5... | collective-permute-start | bytes 1990664 | tf_op jit(solution)/shard_map/ppermute | solution.py:60
  254.5 48.3 %collective-permute-start.41 = (bf16[2,144,1152]{2,1,0:T(8,128)(2,1)S(1)}, bf16[2,144,1152]{2,1,0:T(8,128)(2,1)}, u32[]{:S(2)}, u32[]{:S(2)}) collective-permute-start(bf16[2,144,1152]{2,1,0:T(8,128)(2,1)S(1)} %pad_maximum_fusion.3.refs_0_), channel_id=1, source_target_pairs={{0,16},{4,20},{8,24},{12,28},{16,0},{20,4},{24,8},{28,12},{1,17},{... | collective-permute-start | bytes 1990664 | tf_op jit(solution)/shard_map/ppermute | solution.py:60
  255.7 48.0 %collective-permute-start.38 = (bf16[2,144,1152]{2,1,0:T(8,128)(2,1)S(1)}, bf16[2,144,1152]{2,1,0:T(8,128)(2,1)}, u32[]{:S(2)}, u32[]{:S(2)}) collective-permute-start(bf16[2,144,1152]{2,1,0:T(8,128)(2,1)S(1)} %pad_maximum_fusion.3.refs_0_), channel_id=1, source_target_pairs={{0,4},{4,0},{8,12},{12,8},{16,20},{20,16},{24,28},{28,24},{1,5},{5... | collective-permute-start | bytes 1990664 | tf_op jit(solution)/shard_map/ppermute | solution.py:60
  261.3 60.1 %collective-permute-start.56 = (bf16[2,144,1152]{2,1,0:T(8,128)(2,1)S(1)}, bf16[2,144,1152]{2,1,0:T(8,128)(2,1)}, u32[]{:S(2)}, u32[]{:S(2)}) collective-permute-start(bf16[2,144,1152]{2,1,0:T(8,128)(2,1)S(1)} %pad_maximum_fusion.5.refs_0_), channel_id=1, source_target_pairs={{0,8},{4,12},{8,0},{12,4},{16,24},{20,28},{24,16},{28,20},{1,9},{5... | collective-permute-start | bytes 1990664 | tf_op jit(solution)/shard_map/ppermute | solution.py:60
  262.1 59.4 %collective-permute-start.58 = (bf16[2,144,1152]{2,1,0:T(8,128)(2,1)S(1)}, bf16[2,144,1152]{2,1,0:T(8,128)(2,1)}, u32[]{:S(2)}, u32[]{:S(2)}) collective-permute-start(bf16[2,144,1152]{2,1,0:T(8,128)(2,1)S(1)} %pad_maximum_fusion.5.refs_0_), channel_id=1, source_target_pairs={{0,16},{4,20},{8,24},{12,28},{16,0},{20,4},{24,8},{28,12},{1,17},{... | collective-permute-start | bytes 1990664 | tf_op jit(solution)/shard_map/ppermute | solution.py:60
  580.6 330.2 %collective-permute-start.98 = (bf16[4,4,144,1152]{3,2,1,0:T(8,128)(2,1)}, bf16[4,4,144,1152]{3,2,1,0:T(8,128)(2,1)}, u32[]{:S(2)}, u32[]{:S(2)}) collective-permute-start(bf16[4,4,144,1152]{3,2,1,0:T(8,128)(2,1)} %gradient.21), channel_id=1, source_target_pairs={{0,4},{4,0},{8,12},{12,8},{16,20},{20,16},{24,28},{28,24},{1,5},{5... | collective-permute-start | bytes 15925256 | tf_op jit(solution)/shard_map/ppermute | solution.py:60
  600.8 326.0 %collective-permute-start.90 = (bf16[4,4,144,1152]{3,2,1,0:T(8,128)(2,1)}, bf16[4,4,144,1152]{3,2,1,0:T(8,128)(2,1)}, u32[]{:S(2)}, u32[]{:S(2)}) collective-permute-start(bf16[4,4,144,1152]{3,2,1,0:T(8,128)(2,1)} %gradient.18), channel_id=1, source_target_pairs={{0,4},{4,0},{8,12},{12,8},{16,20},{20,16},{24,28},{28,24},{1,5},{5... | collective-permute-start | bytes 15925256 | tf_op jit(solution)/shard_map/ppermute | solution.py:60
  616.9 128.7 %collective-permute-start.71 = (bf16[512,1152]{0,1:T(8,128)(2,1)}, bf16[512,1152]{0,1:T(8,128)(2,1)}, u32[]{:S(2)}, u32[]{:S(2)}) collective-permute-start(bf16[512,1152]{0,1:T(8,128)(2,1)} %get-tuple-element.133), channel_id=1, source_target_pairs={{1,0},{2,1},{3,2},{5,4},{6,5},{7,6},{9,8},{10,9},{11,10},{13,12},{... | collective-permute-start | bytes 3538952 | tf_op jit(solution)/shard_map/ppermute | solution.py:55
  618.1 128.0 %collective-permute-start.72 = (bf16[512,1152]{0,1:T(8,128)(2,1)}, bf16[512,1152]{0,1:T(8,128)(2,1)}, u32[]{:S(2)}, u32[]{:S(2)}) collective-permute-start(bf16[512,1152]{0,1:T(8,128)(2,1)} %get-tuple-element.134), channel_id=1, source_target_pairs={{0,1},{1,2},{2,3},{4,5},{5,6},{6,7},{8,9},{9,10},{10,11},{12,13},{... | collective-permute-start | bytes 3538952 | tf_op jit(solution)/shard_map/ppermute | solution.py:55
  656.5 87.9 %collective-permute-start.73 = (bf16[256,1152]{0,1:T(8,128)(2,1)}, bf16[256,1152]{0,1:T(8,128)(2,1)}, u32[]{:S(2)}, u32[]{:S(2)}) collective-permute-start(bf16[256,1152]{0,1:T(8,128)(2,1)} %slice.427), channel_id=1, source_target_pairs={{0,2},{1,3},{2,0},{3,1},{4,6},{5,7},{6,4},{7,5},{8,10},{9,11},{10,... | collective-permute-start | bytes 1769480 | tf_op jit(solution)/shard_map/ppermute | solution.py:49
  744.4 87.9 %collective-permute-start.82 = (bf16[4,4,144,288]{3,2,1,0:T(8,128)(2,1)}, bf16[4,4,144,288]{3,2,1,0:T(8,128)(2,1)}, u32[]{:S(2)}, u32[]{:S(2)}) collective-permute-start(bf16[4,4,144,288]{3,2,1,0:T(8,128)(2,1)} %gradient.15), channel_id=1, source_target_pairs={{0,4},{4,0},{8,12},{12,8},{16,20},{20,16},{24,28},{28,24},{1,5},{5... | collective-permute-start | bytes 3981320 | tf_op jit(solution)/shard_map/ppermute | solution.py:60
  745.5 94.2 %collective-permute-start.74 = (bf16[4,4,144,864]{3,2,1,0:T(8,128)(2,1)}, bf16[4,4,144,864]{3,2,1,0:T(8,128)(2,1)}, u32[]{:S(2)}, u32[]{:S(2)}) collective-permute-start(bf16[4,4,144,864]{3,2,1,0:T(8,128)(2,1)} %gradient.12), channel_id=1, source_target_pairs={{0,4},{4,0},{8,12},{12,8},{16,20},{20,16},{24,28},{28,24},{1,5},{5... | collective-permute-start | bytes 11943944 | tf_op jit(solution)/shard_map/ppermute | solution.py:60
  932.3 54.0 %collective-permute-start.91 = (bf16[2,2,144,1152]{3,2,1,0:T(8,128)(2,1)S(1)}, bf16[2,2,144,1152]{3,2,1,0:T(8,128)(2,1)}, u32[]{:S(2)}, u32[]{:S(2)}) collective-permute-start(bf16[2,2,144,1152]{3,2,1,0:T(8,128)(2,1)S(1)} %get-tuple-element.48), channel_id=1, source_target_pairs={{0,16},{4,20},{8,24},{12,28},{16,0},{20,4},{24,8},{28,12},{1,17},{... | collective-permute-start | bytes 3981320 | tf_op jit(solution)/shard_map/ppermute | solution.py:60
  938.7 46.2 %collective-permute-start.93 = (bf16[2,2,144,1152]{3,2,1,0:T(8,128)(2,1)S(1)}, bf16[2,2,144,1152]{3,2,1,0:T(8,128)(2,1)S(1)}, u32[]{:S(2)}, u32[]{:S(2)}) collective-permute-start(bf16[2,2,144,1152]{3,2,1,0:T(8,128)(2,1)S(1)} %get-tuple-element.50), channel_id=1, source_target_pairs={{0,8},{4,12},{8,0},{12,4},{16,24},{20,28},{24,16},{28,20},{1,9},{5... | collective-permute-start | bytes 3981320 | tf_op jit(solution)/shard_map/ppermute | solution.py:60
  949.8 64.1 %collective-permute-start.100 = (bf16[2,144,1152]{2,1,0:T(8,128)(2,1)S(1)}, bf16[2,144,1152]{2,1,0:T(8,128)(2,1)S(1)}, u32[]{:S(2)}, u32[]{:S(2)}) collective-permute-start(bf16[2,144,1152]{2,1,0:T(8,128)(2,1)S(1)} %fusion.45), channel_id=1, source_target_pairs={{0,8},{4,12},{8,0},{12,4},{16,24},{20,28},{24,16},{28,20},{1,9},{5... | collective-permute-start | bytes 1990664 | tf_op jit(solution)/shard_map/ppermute | solution.py:60
  (174 other events, 3078.3 us)
